TPU v7x, 256 devices: a whole 4x4x8 slice. The times are simulated.
256 devices in a mesh: az: 64 (over x, y_hi, z), ax: 4 (over y_lo, core).
Axes of the slice: x: 4, y: 4 (y_hi: 2, y_lo: 2; y = y_hi * 2 + y_lo), z: 8, core: 2. Of those that a mesh axis runs over, the one named last changes fastest.
Arguments:
- fields: float32 [5, 64, 1024, 512], P(None, 'ax', 'az'), may hold values from -6.5 to 6.5, as said below
Outputs:
- advanced: float32 [5, 64, 1024, 512], P(None, 'ax', 'az')
Inputs may be any that keep to these rules, and one draw needn't show every extreme that they name: `fields`: each field is a rough part plus, on every axial plane and cycle, a constant and a first azimuthal harmonic.
All inputs are finite; a program needn't handle non-finite values.
Results may differ from a plain program's by a relative error of at most 0.0003.
Values sent between devices are 32-bit elements; how exact they have to be, the bound alone decides.
A program may use at most 128 MiB of HBM per device.

v0:
```python
import jax
import jax.numpy as jnp
from jax import lax
from jax.sharding import PartitionSpec as P

NEAR = 40
viscosity = 0.2
time_step = 0.1
buoyancy = 1.0


def swapped(block, axis, distance):
    count = lax.axis_size(axis)
    route = []
    for low in range(count):
        high = low | 1 << distance
        if high != low and high < count:
            route += [(low, high), (high, low)]
    return lax.ppermute(block, axis, route)


def with_halo(block, sides, width, periodic):
    for axis, dim in sides:
        count = lax.axis_size(axis)
        forward = [(i, i + 1) for i in range(count - 1)]
        if periodic:
            forward.append((count - 1, 0))
        backward = [(target, source) for source, target in forward]
        low = lax.ppermute(
            lax.slice_in_dim(block, block.shape[dim] - width, None, axis=dim), axis, forward
        )
        high = lax.ppermute(lax.slice_in_dim(block, 0, width, axis=dim), axis, backward)
        block = jnp.concatenate([low, block, high], axis=dim)
    return block


def mode_tables(theta_index, total_theta, modes):
    column = jnp.arange(modes, dtype=jnp.int32)
    product = theta_index[:, None] * column[None, :] % total_theta
    angle = product.astype(jnp.float32) * (2.0 * jnp.pi / total_theta)
    cosine = jnp.cos(angle)
    sine = jnp.sin(angle)
    weight = jnp.where(column == 0, 1.0, 2.0).astype(jnp.float32) / total_theta
    forward = jnp.concatenate([cosine * weight[None, :], sine * (2.0 / total_theta)], axis=1)
    inverse = jnp.concatenate([cosine, sine], axis=1)
    return (forward, inverse)


def cycle_mask(cycles, modes):
    cycle_index = jnp.arange(cycles, dtype=jnp.int32)
    cutoff = jnp.minimum(355 * (2 * cycle_index + 1) // 226, modes - 1)
    column = jnp.arange(modes, dtype=jnp.int32)
    keep = (column[None, :] <= cutoff[:, None]).astype(jnp.float32)
    return jnp.concatenate([keep, keep], axis=1)


def operators(
    center, radial_plus, radial_minus, theta_plus, theta_minus, axial_plus, axial_minus, total_theta
):
    radius = jnp.arange(center.shape[-1], dtype=jnp.float32) + 0.5
    step_angle = 2.0 * jnp.pi / total_theta
    d_radial = (radial_plus - radial_minus) * 0.5
    d_theta = (theta_plus - theta_minus) / (2.0 * step_angle)
    d_axial = (axial_plus - axial_minus) * 0.5
    laplace = (
        radial_plus - 2.0 * center + radial_minus + (radial_plus - radial_minus) / (2.0 * radius)
    )
    laplace = laplace + (theta_plus - 2.0 * center + theta_minus) / (
        radius * radius * step_angle * step_angle
    )
    laplace = laplace + axial_plus - 2.0 * center + axial_minus
    return (d_radial, d_theta, d_axial, laplace)


def on_device(fields):
    count_fields, planes, theta_dev, radial = fields.shape
    sectors = lax.axis_size("az")
    total_theta = theta_dev * sectors
    modes = min(128, total_theta // 2)
    sector = lax.axis_index("az")
    own_index = sector * theta_dev + jnp.arange(theta_dev, dtype=jnp.int32)
    own_forward, own_inverse = mode_tables(own_index, total_theta, modes)
    inner_cycles = fields[:, :, :, :NEAR]
    kept = None
    piece = lax.all_gather(inner_cycles, "az", axis=2, tiled=True)
    piece_index = jnp.arange(piece.shape[2], dtype=jnp.int32)
    piece_forward, unused_inverse = mode_tables(piece_index, total_theta, modes)
    spectra = jnp.einsum("fztj,tc->fzjc", piece, piece_forward, precision=lax.Precision.HIGHEST)
    kept = spectra * cycle_mask(NEAR, modes)[None, None]
    smoothed = jnp.einsum("fzjc,tc->fztj", kept, own_inverse, precision=lax.Precision.HIGHEST)
    state = jnp.concatenate([smoothed, fields[:, :, :, NEAR:]], axis=3)
    flip = jnp.array([-1.0, -1.0, 1.0, 1.0, 1.0], dtype=jnp.float32)[:, None, None]
    top_bit = sectors.bit_length() - 1
    opposite = swapped(state[:, :, :, 0], "az", top_bit - 1)
    opposite = opposite * flip
    theta_padded = with_halo(state, (("az", 2),), 1, True)
    axial_padded = with_halo(state, (("ax", 1),), 1, False)
    radial_plus = jnp.concatenate([state[:, :, :, 1:], jnp.zeros_like(state[:, :, :, :1])], axis=3)
    radial_minus = jnp.concatenate([opposite[:, :, :, None], state[:, :, :, :-1]], axis=3)
    d_radial, d_theta, d_axial, laplace = operators(
        state,
        radial_plus,
        radial_minus,
        theta_padded[:, :, 2:, :],
        theta_padded[:, :, :-2, :],
        axial_padded[:, 2:, :, :],
        axial_padded[:, :-2, :, :],
        total_theta,
    )
    radius = jnp.arange(radial, dtype=jnp.float32) + 0.5
    radial_u = state[0]
    theta_u = state[1]
    axial_u = state[2]
    change = (
        -(radial_u[None] * d_radial + (theta_u / radius)[None] * d_theta + axial_u[None] * d_axial)
        + viscosity * laplace
    )
    inverse_square = 1.0 / (radius * radius)
    first = (
        change[0]
        + theta_u * theta_u / radius
        - viscosity * (radial_u * inverse_square + 2.0 * inverse_square * d_theta[1])
    )
    second = (
        change[1]
        - radial_u * theta_u / radius
        - viscosity * (theta_u * inverse_square - 2.0 * inverse_square * d_theta[0])
    )
    third = change[2] + buoyancy * state[3]
    change = jnp.concatenate([first[None], second[None], third[None], change[3:]], axis=0)
    return state + time_step * change


def solution(mesh):
    placed = (P(None, "ax", "az", None),)
    return jax.shard_map(
        on_device, mesh=mesh, in_specs=placed, out_specs=P(None, "ax", "az", None), check_vma=False
    )
```

profile of v0, /device:TPU:1, one launch (start us, length us, event | category | flops | bytes accessed | tf_op | source)
XLA Modules:
  0.0 499.4 jit_solution(17314941103463150801)
XLA Ops:
  6.5 2.0 slice.73
  8.6 4.0 slice.74
  12.5 3.2 copy.19
  15.9 0.1 iota_compare_fusion
  16.0 0.1 fusion.43
  16.1 3.0 sine_multiply_fusion
  19.1 355.6 %all-gather.2.cloned.1.call-done = f32[5,16,1024,40]{3,2,1,0:T(8,128)} async-done(((f32[5,16,16,40]{3,2,1,0:T(8,128)}), f32[5,16,1024,40]{3,2,1,0:T(8,128)}) %all-gather.2.cloned.1.call-update) | async-done | bytes 13107216 | tf_op jit(solution)/shard_map/all_gather | solution.py:85
  374.7 70.2 %fusion.8 = f32[256,5,16,40]{0,3,2,1:T(8,128)S(1)} fusion(f32[5,16,1024,40]{3,2,1,0:T(8,128)} %all-gather.2.cloned.1.call-done, f32[1024,128]{1,0:T(8,128)S(1)} %get-tuple-element.19, f32[1024,128]{1,0:T(8,128)} %get-tuple-element.20), kind=kOutput, calls=%fused_computation.40 | convolution fusion | flops 10066591744 | bytes 17432576 | tf_op jit(solution)/shard_map/fztj,tc->fzjc/dot_general | solution.py:88
  444.9 5.4 %fusion.7 = f32[5,16,16,40]{3,2,1,0:T(8,128)S(1)} fusion(f32[256,5,16,40]{0,3,2,1:T(8,128)S(1)} %fusion.8, f32[40,256]{1,0:T(8,128)S(1)} %add_convert_fusion, f32[16,128]{1,0:T(8,128)S(1)} %get-tuple-element.18, f32[16,128]{1,0:T(8,128)S(1)} %get-tuple-element.17), kind=kOutput, calls=%fused_computation.38 | convolution fusion | flops 158109696 | bytes 3538944 | tf_op jit(solution)/shard_map/fzjc,tc->fztj/dot_general | solution.py:90
  450.3 0.2 copy.10
  450.5 0.9 fusion.33
  451.4 3.9 fusion.1
  455.3 0.2 slice_reduce_fusion
  455.6 1.6 multiply_bitcast_fusion.1
  457.2 2.7 collective-permute-start
  459.9 0.7 fusion.31
  460.6 2.3 collective-permute-start.1
  462.9 0.7 copy.12
  463.6 6.0 %collective-permute-start.3 = (f32[5,1,16,512]{3,2,1,0:T(8,128)}, f32[5,1,16,512]{3,2,1,0:T(8,128)}, u32[]{:S(2)}, u32[]{:S(2)}) collective-permute-start(f32[5,1,16,512]{3,2,1,0:T(8,128)} %copy.12), channel_id=1, source_target_pairs={{1,0},{2,1},{3,2},{5,4},{6,5},{7,6},{9,8},{10,9},{11,10},{13,12},{... | collective-permute-start | bytes 491528 | tf_op jit(solution)/shard_map/ppermute | solution.py:32
  469.6 0.7 copy.14
  470.2 3.0 collective-permute-start.4
  473.3 0.1 multiply_bitcast_fusion.2
  473.3 1.4 copy.11
  474.7 1.3 collective-permute-done.3
  476.0 1.1 copy.13
  477.1 1.1 copy.15
  478.2 7.4 %multiply_add_fusion = f32[5,16,16,512]{3,1,2,0:T(8,128)S(1)} fusion(f32[5,1,16,512]{3,1,2,0:T(1,128)S(1)} %copy.13, f32[5,16,16,472]{3,1,2,0:T(8,128)S(1)} %copy.19, f32[5,16,16,40]{3,1,2,0:T(8,128)S(1)} %copy.10, f32[5,1,16,512]{3,1,2,0:T(1,128)S(1)} %copy.15, f32[5,16,16,511]{3,1,2,0:T(8,128)} %get-tuple-element.14, f32[5,16,16,1]{3,1,2,0:T(8,128)} %copy.11, ...), kind=kLoop, calls=%fused_computation.26 | loop fusion | flops 21626880 | bytes 12712960 | tf_op jit(solution)/shard_map/add | solution.py:115
  485.6 0.1 slice.122
  485.7 2.3 fusion.6
  488.0 0.8 fusion.26
  488.8 0.8 fusion.3
  489.6 3.0 copy.16
  (16 shorter events, 0.1 us)
Async XLA Ops:
  6.5 368.2 %all-gather.2.cloned.1.call-start = ((), (), s32[]{:S(2)}) async-start(), calls=%async_computation | async-start | bytes 42598400 | tf_op jit(solution)/shard_map/all_gather | solution.py:85
  457.2 16.1 %copy-start = (f32[5]{0:T(128)S(1)}, f32[5]{0:T(128)}, u32[]{:S(2)}) copy-start(f32[5]{0:T(128)} %constant.82.clone) | copy-start | bytes 64
  457.2 16.1 %collective-permute-start = (f32[5,16,16]{2,1,0:T(8,128)S(1)}, f32[5,16,16]{2,1,0:T(8,128)S(1)}, u32[]{:S(2)}, u32[]{:S(2)}) collective-permute-start(f32[5,16,16]{2,1,0:T(8,128)S(1)} %slice_reduce_fusion), channel_id=1, source_target_pairs={{0,128},{128,0},{4,132},{132,4},{8,136},{136,8},{12,140},{140,12},... | collective-permute-start | bytes 15368 | tf_op jit(solution)/shard_map/ppermute | solution.py:19
  460.6 17.6 %collective-permute-start.1 = (f32[5,16,1,512]{3,1,2,0:T(8,128)}, f32[5,16,1,512]{3,1,2,0:T(8,128)S(1)}, u32[]{:S(2)}, u32[]{:S(2)}) collective-permute-start(f32[5,16,1,512]{3,1,2,0:T(8,128)} %get-tuple-element.12), channel_id=1, source_target_pairs={{4,0},{8,4},{12,8},{16,12},{20,16},{24,20},{28,24},{32,28},{36,32}... | collective-permute-start | bytes 491528 | tf_op jit(solution)/shard_map/ppermute | solution.py:32
  462.9 15.3 %collective-permute-start.2 = (f32[5,16,1,512]{3,1,2,0:T(8,128)}, f32[5,16,1,512]{3,1,2,0:T(8,128)}, u32[]{:S(2)}, u32[]{:S(2)}) collective-permute-start(f32[5,16,1,512]{3,1,2,0:T(8,128)} %get-tuple-element.11), channel_id=1, source_target_pairs={{0,4},{4,8},{8,12},{12,16},{16,20},{20,24},{24,28},{28,32},{32,36}... | collective-permute-start | bytes 491528 | tf_op jit(solution)/shard_map/ppermute | solution.py:29
  463.6 12.4 %collective-permute-start.3 = (f32[5,1,16,512]{3,2,1,0:T(8,128)}, f32[5,1,16,512]{3,2,1,0:T(8,128)}, u32[]{:S(2)}, u32[]{:S(2)}) collective-permute-start(f32[5,1,16,512]{3,2,1,0:T(8,128)} %copy.12), channel_id=1, source_target_pairs={{1,0},{2,1},{3,2},{5,4},{6,5},{7,6},{9,8},{10,9},{11,10},{13,12},{... | collective-permute-start | bytes 491528 | tf_op jit(solution)/shard_map/ppermute | solution.py:32
  470.2 6.9 %collective-permute-start.4 = (f32[5,1,16,512]{3,2,1,0:T(8,128)}, f32[5,1,16,512]{3,2,1,0:T(8,128)}, u32[]{:S(2)}, u32[]{:S(2)}) collective-permute-start(f32[5,1,16,512]{3,2,1,0:T(8,128)} %copy.14), channel_id=1, source_target_pairs={{0,1},{1,2},{2,3},{4,5},{5,6},{6,7},{8,9},{9,10},{10,11},{12,13},{... | collective-permute-start | bytes 491528 | tf_op jit(solution)/shard_map/ppermute | solution.py:29
Sparse Core Ops, SparseCore 0:
  10.8 363.8 all-gather.1
where the time goes:
time: 500 us; the launch traced here: 499 us
  waiting for transfers between devices  357 us (71%)
  matrix products  75.6 us (15%)
  other arithmetic  21.8 us (4%)
  local copies, waits for them, and re-layouts  17.6 us (4%)
  starting transfers between devices  13.9 us (3%)
  between operations  13.6 us (3%)
    all_gather x1, waiting for transfers between devices, on_device(): piece = lax.all_gather(inner_cycles, 'az', axis=2, tiled=True)  356 us
    dot_general x1, matrix products, on_device(): jnp.einsum('fztj,tc->fzjc', piece, piece_forward, precision=lax.Precision...  70.2 us
  transfers between devices with their start and end apart: 6, of which 2 were waited for; matrix products, arithmetic and copies ran while one was open for 3% of the time, Pallas kernels for 0%

commit v1 on v0

--- a/solution.py
+++ b/solution.py
@@ -82,7 +82,9 @@
     own_forward, own_inverse = mode_tables(own_index, total_theta, modes)
     inner_cycles = fields[:, :, :, :NEAR]
     kept = None
-    piece = lax.all_gather(inner_cycles, "az", axis=2, tiled=True)
+    piece = jnp.concatenate(
+        lax.all_to_all(jnp.stack([inner_cycles] * lax.axis_size("az")), "az", 0, 0), axis=2
+    )
     piece_index = jnp.arange(piece.shape[2], dtype=jnp.int32)
     piece_forward, unused_inverse = mode_tables(piece_index, total_theta, modes)
     spectra = jnp.einsum("fztj,tc->fzjc", piece, piece_forward, precision=lax.Precision.HIGHEST)

time: 500 us -> 642 us (1.28); the launches traced: 499 us -> 632 us
  local copies, waits for them, and re-layouts: 17.6 us -> 181 us
  waiting for transfers between devices: 357 us -> 273 us
  other arithmetic: 21.8 us -> 61.4 us
  starting transfers between devices: 13.9 us -> 40.3 us
  between operations: 13.6 us -> 0.43 us
    all_gather x1 -> x0, waiting for transfers between devices: 356 us -> none  [on_device(): piece = lax.all_gather(inner_cycles, 'az', axis=2, tiled=True)]
    all_to_all x0 -> x1, waiting for transfers between devices: none -> 273 us  [on_device(): lax.all_to_all(jnp.stack([inner_cycles] * lax.axis_size('az')), 'az', 0, 0)]
    unnamed x3 -> x9, local copies, waits for them, and re-layouts: 3.25 us -> 126 us
    all_to_all x0 -> x1, other arithmetic: none -> 39.7 us  [on_device(): lax.all_to_all(jnp.stack([inner_cycles] * lax.axis_size('az')), 'az', 0, 0)]
    reshape x0 -> x1, local copies, waits for them, and re-layouts: none -> 28.6 us  [on_device(): jnp.concatenate(lax.all_to_all(jnp.stack([inner_cycles] * lax.axis_size('...]
    all_to_all x0 -> x1, starting transfers between devices: none -> 15.5 us  [on_device(): lax.all_to_all(jnp.stack([inner_cycles] * lax.axis_size('az')), 'az', 0, 0)]
    another operation x0 -> x1, local copies, waits for them, and re-layouts: none -> 13.9 us  [on_device(): jnp.stack([inner_cycles] * lax.axis_size('az'))]
    ppermute x2, starting transfers between devices: 8.24 us -> 19.3 us  [with_halo(): lax.ppermute(lax.slice_in_dim(block, 0, width, axis=dim), axis, backward)]
  transfers between devices with their start and end apart: 6 -> 6, of which waited for: 2 -> 1; matrix products, arithmetic and copies ran while one was open for 3% -> 2% of each run, Pallas kernels for 0% -> 0%
where the time goes in v1:
time: 642 us; the launch traced here: 632 us
  waiting for transfers between devices  273 us (43%)
  local copies, waits for them, and re-layouts  181 us (28%)
  matrix products  75.8 us (12%)
  other arithmetic  61.4 us (10%)
  starting transfers between devices  40.3 us (6%)
    all_to_all x1, waiting for transfers between devices, on_device(): lax.all_to_all(jnp.stack([inner_cycles] * lax.axis_size('az')), 'az', 0, 0)  273 us
    unnamed x9, local copies, waits for them, and re-layouts  126 us
    dot_general x1, matrix products, on_device(): jnp.einsum('fztj,tc->fzjc', piece, piece_forward, precision=lax.Precision...  70.4 us
    all_to_all x1, other arithmetic, on_device(): lax.all_to_all(jnp.stack([inner_cycles] * lax.axis_size('az')), 'az', 0, 0)  39.7 us
    reshape x1, local copies, waits for them, and re-layouts, on_device(): jnp.concatenate(lax.all_to_all(jnp.stack([inner_cycles] * lax.axis_size('...  28.6 us
    ppermute x2, starting transfers between devices, with_halo(): lax.ppermute(lax.slice_in_dim(block, 0, width, axis=dim), axis, backward)  19.3 us
    all_to_all x1, starting transfers between devices, on_device(): lax.all_to_all(jnp.stack([inner_cycles] * lax.axis_size('az')), 'az', 0, 0)  15.5 us
    another operation x1, local copies, waits for them, and re-layouts, on_device(): jnp.stack([inner_cycles] * lax.axis_size('az'))  13.9 us
  transfers between devices with their start and end apart: 6, of which 1 were waited for; matrix products, arithmetic and copies ran while one was open for 2% of the time, Pallas kernels for 0%

profile of v1, /device:TPU:1, one launch (start us, length us, event | category | flops | bytes accessed | tf_op | source)
XLA Modules:
  0.0 632.3 jit_solution(12535912475822221283)
XLA Ops:
  0.0 1.1 slice.73
  1.1 13.9 %stack.2 = f32[64,5,16,16,40]{4,3,2,1,0:T(8,128)} broadcast(f32[5,16,16,40]{3,2,1,0:T(8,128)S(1)} %slice.73), dimensions={1,2,3,4} | broadcast | bytes 13312000 | tf_op jit(solution)/shard_map/stack | solution.py:86
  15.1 58.5 %reshape.66 = f32[64,1,51200]{2,1,0:T(1,128)} reshape(f32[64,5,16,16,40]{4,3,2,1,0:T(8,128)} %stack.2) | data formatting | bytes 26214400
  73.6 15.5 %all-to-all-start = ((f32[64,1,51200]{2,1,0:T(1,128)}), f32[64,1,51200]{2,1,0:T(1,128)}, u32[]{:S(2)}, u32[]{:S(2)}) async-start(f32[64,1,51200]{2,1,0:T(1,128)} %reshape.66), calls=%async_computation | async-start | bytes 26214400 | tf_op jit(solution)/shard_map/all_to_all | solution.py:86
  89.1 2.2 slice.74
  91.3 3.2 copy.24
  94.9 3.0 sine_multiply_fusion
  97.8 273.3 %all-to-all-done = f32[64,1,51200]{2,1,0:T(1,128)} async-done(((f32[64,1,51200]{2,1,0:T(1,128)}), f32[64,1,51200]{2,1,0:T(1,128)}, u32[]{:S(2)}, u32[]{:S(2)}) %all-to-all-start) | async-done | bytes 13107232 | tf_op jit(solution)/shard_map/all_to_all | solution.py:86
  371.1 0.6 broadcast.180
  371.7 39.7 %reduce.2 = f32[64,51200]{1,0:T(8,128)} reduce(f32[64,1,51200]{2,1,0:T(1,128)} %all-to-all-done, f32[]{:T(128)} %broadcast.180), dimensions={1}, to_apply=%all_to_all.3.reduce_sub_computation | reduce | bytes 26214404 | tf_op jit(solution)/shard_map/all_to_all | solution.py:86
  411.3 64.3 %reshape.67 = f32[64,5,16,16,40]{4,3,2,1,0:T(8,128)} reshape(f32[64,51200]{1,0:T(8,128)} %reduce.2) | data formatting | bytes 26214400
  475.7 28.6 %copy.11 = f32[5,16,64,16,40]{4,3,2,1,0:T(8,128)} copy(f32[5,16,64,16,40]{4,3,1,0,2:T(8,128)} %bitcast.29) | data formatting | bytes 26214400 | tf_op jit(solution)/shard_map/reshape | solution.py:85
  504.3 70.4 %fusion.8 = f32[256,5,16,40]{0,3,2,1:T(8,128)S(1)} fusion(f32[5,16,1024,40]{3,2,1,0:T(8,128)} %bitcast.28, f32[1024,128]{1,0:T(8,128)S(1)} %get-tuple-element.19, f32[1024,128]{1,0:T(8,128)S(1)} %copy-done.1), kind=kOutput, calls=%fused_computation.40 | convolution fusion | flops 10066591744 | bytes 17432576 | tf_op jit(solution)/shard_map/fztj,tc->fzjc/dot_general | solution.py:90
  574.7 5.4 fusion.7
  580.4 0.9 fusion.33
  581.3 4.0 fusion.1
  585.5 1.6 multiply_bitcast_fusion.1
  587.1 3.3 collective-permute-start
  590.4 0.7 fusion.31
  591.2 14.3 %collective-permute-start.1 = (f32[5,16,1,512]{3,1,2,0:T(8,128)}, f32[5,16,1,512]{3,1,2,0:T(8,128)S(1)}, u32[]{:S(2)}, u32[]{:S(2)}) collective-permute-start(f32[5,16,1,512]{3,1,2,0:T(8,128)} %get-tuple-element.12), channel_id=1, source_target_pairs={{4,0},{8,4},{12,8},{16,12},{20,16},{24,20},{28,24},{32,28},{36,32}... | collective-permute-start | bytes 491528 | tf_op jit(solution)/shard_map/ppermute | solution.py:32
  605.5 0.7 copy.16
  606.2 4.9 collective-permute-start.3
  611.1 0.7 copy.18
  611.8 2.2 collective-permute-start.4
  614.1 1.4 copy.15
  615.5 1.1 copy.17
  616.6 1.1 copy.19
  617.7 7.4 %multiply_add_fusion = f32[5,16,16,512]{3,1,2,0:T(8,128)S(1)} fusion(f32[5,1,16,512]{3,1,2,0:T(1,128)S(1)} %copy.17, f32[5,16,16,472]{3,1,2,0:T(8,128)S(1)} %copy.24, f32[5,16,16,40]{3,1,2,0:T(8,128)S(1)} %copy.14, f32[5,1,16,512]{3,1,2,0:T(1,128)S(1)} %copy.19, f32[5,16,16,511]{3,1,2,0:T(8,128)} %get-tuple-element.14, f32[5,16,16,1]{3,1,2,0:T(8,128)} %copy.15, ...), kind=kLoop, calls=%fused_computation.26 | loop fusion | flops 21626880 | bytes 12712960 | tf_op jit(solution)/shard_map/add | solution.py:117
  625.1 2.3 fusion.6
  627.4 0.8 fusion.26
  628.2 0.8 fusion.3
  629.1 3.0 copy.20
  (25 shorter events, 0.9 us)
Async XLA Ops:
  73.6 15.5 %copy-start = (f32[5,16,16,512]{3,2,1,0:T(8,128)S(1)}, f32[5,16,16,512]{3,2,1,0:T(8,128)}, u32[]{:S(2)}) copy-start(f32[5,16,16,512]{3,2,1,0:T(8,128)} %param.2) | copy-start | bytes 7864324
  73.6 297.5 %all-to-all-start = ((f32[64,1,51200]{2,1,0:T(1,128)}), f32[64,1,51200]{2,1,0:T(1,128)}, u32[]{:S(2)}, u32[]{:S(2)}) async-start(f32[64,1,51200]{2,1,0:T(1,128)} %reshape.66), calls=%async_computation | async-start | bytes 26214400 | tf_op jit(solution)/shard_map/all_to_all | solution.py:86
  475.7 28.6 %copy-start.1 = (f32[1024,128]{1,0:T(8,128)S(1)}, f32[1024,128]{1,0:T(8,128)}, u32[]{:S(2)}) copy-start(f32[1024,128]{1,0:T(8,128)} %get-tuple-element.20) | copy-start | bytes 1572868
  587.1 26.9 %copy-start.2 = (f32[5]{0:T(128)S(1)}, f32[5]{0:T(128)}, u32[]{:S(2)}) copy-start(f32[5]{0:T(128)} %constant.82.clone) | copy-start | bytes 64
  587.1 26.9 %collective-permute-start = (f32[5,16,16]{2,1,0:T(8,128)S(1)}, f32[5,16,16]{2,1,0:T(8,128)S(1)}, u32[]{:S(2)}, u32[]{:S(2)}) collective-permute-start(f32[5,16,16]{2,1,0:T(8,128)S(1)} %slice_reduce_fusion), channel_id=1, source_target_pairs={{0,128},{128,0},{4,132},{132,4},{8,136},{136,8},{12,140},{140,12},... | collective-permute-start | bytes 15368 | tf_op jit(solution)/shard_map/ppermute | solution.py:19
  591.2 26.5 %collective-permute-start.1 = (f32[5,16,1,512]{3,1,2,0:T(8,128)}, f32[5,16,1,512]{3,1,2,0:T(8,128)S(1)}, u32[]{:S(2)}, u32[]{:S(2)}) collective-permute-start(f32[5,16,1,512]{3,1,2,0:T(8,128)} %get-tuple-element.12), channel_id=1, source_target_pairs={{4,0},{8,4},{12,8},{16,12},{20,16},{24,20},{28,24},{32,28},{36,32}... | collective-permute-start | bytes 491528 | tf_op jit(solution)/shard_map/ppermute | solution.py:32
  605.5 12.2 %collective-permute-start.2 = (f32[5,16,1,512]{3,1,2,0:T(8,128)}, f32[5,16,1,512]{3,1,2,0:T(8,128)}, u32[]{:S(2)}, u32[]{:S(2)}) collective-permute-start(f32[5,16,1,512]{3,1,2,0:T(8,128)} %get-tuple-element.11), channel_id=1, source_target_pairs={{0,4},{4,8},{8,12},{12,16},{16,20},{20,24},{24,28},{28,32},{32,36}... | collective-permute-start | bytes 491528 | tf_op jit(solution)/shard_map/ppermute | solution.py:29
  606.2 9.3 %collective-permute-start.3 = (f32[5,1,16,512]{3,2,1,0:T(8,128)}, f32[5,1,16,512]{3,2,1,0:T(8,128)}, u32[]{:S(2)}, u32[]{:S(2)}) collective-permute-start(f32[5,1,16,512]{3,2,1,0:T(8,128)} %copy.16), channel_id=1, source_target_pairs={{1,0},{2,1},{3,2},{5,4},{6,5},{7,6},{9,8},{10,9},{11,10},{13,12},{... | collective-permute-start | bytes 491528 | tf_op jit(solution)/shard_map/ppermute | solution.py:32
  611.8 4.8 collective-permute-start.4
